TPU v7x, 512 devices: a whole 4x4x16 slice. The times are simulated.
512 devices in a mesh: grp: 16 (over x_lo, y, core), dev: 32 (over x_hi, z).
Axes of the slice: x: 4 (x_hi: 2, x_lo: 2; x = x_hi * 2 + x_lo), y: 4, z: 16, core: 2. Of those that a mesh axis runs over, the one named last changes fastest.
Arguments:
- voltage: float32 [2, 4096, 4192], P(None, ('grp', 'dev')), may hold values from -6 to 6
- filter_taps: float32 [4, 32], replicated, may hold values from -0.5 to 0.5
- plan: int32 [16, 9], P('grp'), may hold values from 0 to 8, each once within a row
Outputs:
- visibility: bfloat16 [16, 9, 32, 2, 256, 256], P('grp', None, 'dev')
Inputs may be any that keep to these rules, and one draw needn't show every extreme that they name: Each row of plan holds every distance 0 to 8 once.
All inputs are finite; a program needn't handle non-finite values.
Results may differ from a plain program's by a relative error of at most 0.0056.
Values may be sent and summed in bfloat16 or wider, within the bound.
No kernel may reach another device: no remote copies, remote signals or barrier semaphores. Data moves between devices by JAX's collectives and lax.ppermute only.
A program may use at most 64 MiB of HBM per device.

v0:
```python
import math
import jax
import jax.numpy as jnp
from jax import lax
from jax.sharding import PartitionSpec as P

F = 32
TAPS = 4
SPECTRA = 128
FRAMES = 131


def shifted(x, axis, by):
    length = lax.axis_size(axis)
    return lax.ppermute(x, axis, [(i, (i + by) % length) for i in range(length)])


def compute_spectra(voltage, filter_taps):
    signal_input_count = voltage.shape[1]
    framed_samples = voltage.reshape(2, signal_input_count, FRAMES, F)
    filtered = filter_taps[0][None, None, None, :] * framed_samples[:, :, 0:SPECTRA, :]
    for p in range(1, TAPS):
        filtered = (
            filtered
            + filter_taps[p][None, None, None, :] * framed_samples[:, :, p : p + SPECTRA, :]
        )
    indices = jnp.arange(F, dtype=jnp.int32)
    phase_angle = (indices[:, None] * indices[None, :] % F).astype(jnp.float32) * (
        2.0 * math.pi / F
    )
    cosine_table = jnp.cos(phase_angle)
    sine_table = jnp.sin(phase_angle)
    highest = lax.Precision.HIGHEST
    real_part = jnp.einsum(
        "csn,nf->fcs", filtered[0], cosine_table, precision=highest
    ) + jnp.einsum("csn,nf->fcs", filtered[1], sine_table, precision=highest)
    imaginary_component = jnp.einsum(
        "csn,nf->fcs", filtered[1], cosine_table, precision=highest
    ) - jnp.einsum("csn,nf->fcs", filtered[0], sine_table, precision=highest)
    return jnp.stack([real_part, imaginary_component], axis=2).astype(jnp.bfloat16)


def correlate(own_block, partner):
    chans, rows_here = (own_block.shape[0], own_block.shape[1])
    left_spectrum_rows = own_block.reshape(chans, rows_here, -1)
    real_part = partner[:, :, 0, :]
    imaginary_component = partner[:, :, 1, :]
    right_spectrum_rows = jnp.stack(
        [
            jnp.concatenate([real_part, imaginary_component], -1),
            jnp.concatenate([-imaginary_component, real_part], -1),
        ],
        axis=1,
    )
    cross_products = jnp.einsum(
        "gzi,gkvi->gkzv",
        left_spectrum_rows,
        right_spectrum_rows,
        preferred_element_type=jnp.float32,
    )
    return (cross_products / SPECTRA).astype(jnp.bfloat16)


def per_device(voltage, filter_taps, plan):
    local_spectra = compute_spectra(voltage, filter_taps)
    own_block = lax.all_to_all(local_spectra, "dev", split_axis=0, concat_axis=1, tiled=True)
    groups = lax.axis_size("grp")
    rounds = groups // 2 + 1
    results = [correlate(own_block, own_block)]
    received = own_block
    for distance in range(1, rounds):
        received = shifted(own_block, "grp", distance)
        results.append(correlate(own_block, received))
    stacked = jnp.stack(results, axis=0)
    return jnp.take(stacked, plan[0], axis=0)[None]


def solution(mesh):
    return jax.shard_map(
        per_device,
        mesh=mesh,
        in_specs=(P(None, ("grp", "dev"), None), P(), P("grp", None)),
        out_specs=P("grp", None, "dev", None, None, None),
        check_vma=False,
    )
```

profile of v0, /device:TPU:1, one launch (start us, length us, event | category | flops | bytes accessed | tf_op | source)
XLA Modules:
  0.0 89.8 jit_solution(14616734474427329352)
XLA Ops:
  0.0 1.3 %reshape.257 = f32[2,8,131,32]{3,2,1,0:T(8,128)S(1)} reshape(f32[2,8,4192]{2,1,0:T(8,128)} %param.3) | data formatting | bytes 536576 | tf_op jit(solution)/shard_map/reshape | solution.py:20
  1.3 1.8 %fusion.111 = (f32[2,8,128,32]{3,2,1,0:T(8,128)S(1)}, f32[2,8,128,32]{3,2,1,0:T(8,128)}, f32[2,8,128,32]{3,2,1,0:T(8,128)S(1)}, f32[2,8,128,32]{3,2,1,0:T(8,128)}) fusion(f32[2,8,131,32]{3,2,1,0:T(8,128)S(1)} %reshape.257), kind=kLoop, calls=%fused_computation.181 | loop fusion | bytes 2097152 | tf_op jit(solution)/shard_map/slice | solution.py:21
  3.1 0.0 copy-start.1
  3.1 1.5 %copy.22 = f32[2,8,128,32]{2,3,1,0:T(8,128)S(1)} copy(f32[2,8,128,32]{3,2,1,0:T(8,128)} %get-tuple-element.8) | data formatting | bytes 524288
  4.6 1.5 %copy.21 = f32[2,8,128,32]{2,3,1,0:T(8,128)S(1)} copy(f32[2,8,128,32]{3,2,1,0:T(8,128)} %get-tuple-element.6) | data formatting | bytes 524288
  6.2 0.3 copy.20
  6.5 0.0 copy-start.2
  6.5 0.3 copy.19
  6.8 0.0 copy-done.1
  6.8 0.2 multiply_add_fusion
  7.0 0.3 fusion.59
  7.3 0.3 fusion.58
  7.7 0.3 fusion.29
  8.0 0.3 fusion.30
  8.4 0.7 copy.16
  9.1 18.5 %all-to-all-start = ((bf16[32,8,2,128]{3,1,2,0:T(8,128)(2,1)}), bf16[32,8,2,128]{3,1,2,0:T(8,128)(2,1)S(1)}, u32[]{:S(2)}, u32[]{:S(2)}) async-start(bf16[32,8,2,128]{3,1,2,0:T(8,128)(2,1)} %copy.16), calls=%async_computation | async-start | bytes 262144 | tf_op jit(solution)/shard_map/all_to_all | solution.py:66
  27.6 0.0 copy-done.2
  27.6 16.3 %all-to-all-done = bf16[32,8,2,128]{3,1,2,0:T(8,128)(2,1)S(1)} async-done(((bf16[32,8,2,128]{3,1,2,0:T(8,128)(2,1)}), bf16[32,8,2,128]{3,1,2,0:T(8,128)(2,1)S(1)}, u32[]{:S(2)}, u32[]{:S(2)}) %all-to-all-start) | async-done | bytes 131104 | tf_op jit(solution)/shard_map/all_to_all | solution.py:66
  44.0 6.1 %collective-permute-start = (bf16[1,256,2,128]{3,1,2,0:T(8,128)(2,1)S(1)}, bf16[1,256,2,128]{3,1,2,0:T(8,128)(2,1)S(1)}, u32[]{:S(2)}, u32[]{:S(2)}) collective-permute-start(bf16[1,256,2,128]{3,1,2,0:T(8,128)(2,1)S(1)} %bitcast.255), channel_id=1, source_target_pairs={{0,32},{32,64},{64,96},{96,128},{128,160},{160,192},{192,224},{224... | collective-permute-start | bytes 393224 | tf_op jit(solution)/shard_map/ppermute | solution.py:15
  50.1 3.2 %collective-permute-start.1 = (bf16[1,256,2,128]{3,1,2,0:T(8,128)(2,1)S(1)}, bf16[1,256,2,128]{3,1,2,0:T(8,128)(2,1)S(1)}, u32[]{:S(2)}, u32[]{:S(2)}) collective-permute-start(bf16[1,256,2,128]{3,1,2,0:T(8,128)(2,1)S(1)} %bitcast.256), channel_id=1, source_target_pairs={{0,64},{32,96},{64,128},{96,160},{128,192},{160,224},{192,256},{22... | collective-permute-start | bytes 393224 | tf_op jit(solution)/shard_map/ppermute | solution.py:15
  53.3 3.5 %collective-permute-start.2 = (bf16[1,256,2,128]{3,1,2,0:T(8,128)(2,1)S(1)}, bf16[1,256,2,128]{3,1,2,0:T(8,128)(2,1)S(1)}, u32[]{:S(2)}, u32[]{:S(2)}) collective-permute-start(bf16[1,256,2,128]{3,1,2,0:T(8,128)(2,1)S(1)} %bitcast.257), channel_id=1, source_target_pairs={{0,96},{32,128},{64,160},{96,192},{128,224},{160,256},{192,288},{2... | collective-permute-start | bytes 393224 | tf_op jit(solution)/shard_map/ppermute | solution.py:15
  56.8 2.3 %collective-permute-start.3 = (bf16[1,256,2,128]{3,1,2,0:T(8,128)(2,1)S(1)}, bf16[1,256,2,128]{3,1,2,0:T(8,128)(2,1)S(1)}, u32[]{:S(2)}, u32[]{:S(2)}) collective-permute-start(bf16[1,256,2,128]{3,1,2,0:T(8,128)(2,1)S(1)} %bitcast.258), channel_id=1, source_target_pairs={{0,128},{32,160},{64,192},{96,224},{128,256},{160,288},{192,320},{... | collective-permute-start | bytes 393224 | tf_op jit(solution)/shard_map/ppermute | solution.py:15
  59.1 4.7 %collective-permute-start.4 = (bf16[1,256,2,128]{3,1,2,0:T(8,128)(2,1)S(1)}, bf16[1,256,2,128]{3,1,2,0:T(8,128)(2,1)S(1)}, u32[]{:S(2)}, u32[]{:S(2)}) collective-permute-start(bf16[1,256,2,128]{3,1,2,0:T(8,128)(2,1)S(1)} %bitcast.259), channel_id=1, source_target_pairs={{0,160},{32,192},{64,224},{96,256},{128,288},{160,320},{192,352},{... | collective-permute-start | bytes 393224 | tf_op jit(solution)/shard_map/ppermute | solution.py:15
  63.8 0.3 fusion.26
  64.1 0.0 collective-permute-done
  64.1 2.8 %collective-permute-start.5 = (bf16[1,256,2,128]{3,1,2,0:T(8,128)(2,1)S(1)}, bf16[1,256,2,128]{3,1,2,0:T(8,128)(2,1)S(1)}, u32[]{:S(2)}, u32[]{:S(2)}) collective-permute-start(bf16[1,256,2,128]{3,1,2,0:T(8,128)(2,1)S(1)} %bitcast.260), channel_id=1, source_target_pairs={{0,192},{32,224},{64,256},{96,288},{128,320},{160,352},{192,384},{... | collective-permute-start | bytes 393224 | tf_op jit(solution)/shard_map/ppermute | solution.py:15
  67.0 0.0 collective-permute-done.1
  67.0 3.6 %collective-permute-start.6 = (bf16[1,256,2,128]{3,1,2,0:T(8,128)(2,1)S(1)}, bf16[1,256,2,128]{3,1,2,0:T(8,128)(2,1)S(1)}, u32[]{:S(2)}, u32[]{:S(2)}) collective-permute-start(bf16[1,256,2,128]{3,1,2,0:T(8,128)(2,1)S(1)} %bitcast.261), channel_id=1, source_target_pairs={{0,224},{32,256},{64,288},{96,320},{128,352},{160,384},{192,416},{... | collective-permute-start | bytes 393224 | tf_op jit(solution)/shard_map/ppermute | solution.py:15
  70.7 0.0 collective-permute-done.2
  70.7 3.1 %collective-permute-start.7 = (bf16[1,256,2,128]{3,1,2,0:T(8,128)(2,1)S(1)}, bf16[1,256,2,128]{3,1,2,0:T(8,128)(2,1)S(1)}, u32[]{:S(2)}, u32[]{:S(2)}) collective-permute-start(bf16[1,256,2,128]{3,1,2,0:T(8,128)(2,1)S(1)} %bitcast.262), channel_id=1, source_target_pairs={{0,256},{32,288},{64,320},{96,352},{128,384},{160,416},{192,448},{... | collective-permute-start | bytes 393224 | tf_op jit(solution)/shard_map/ppermute | solution.py:15
  73.8 0.0 collective-permute-done.3
  73.9 0.0 collective-permute-done.4
  74.0 0.0 collective-permute-done.5
  74.1 1.4 %collective-permute-done.6 = bf16[1,256,2,128]{3,1,2,0:T(8,128)(2,1)S(1)} collective-permute-done((bf16[1,256,2,128]{3,1,2,0:T(8,128)(2,1)S(1)}, bf16[1,256,2,128]{3,1,2,0:T(8,128)(2,1)S(1)}, u32[]{:S(2)}, u32[]{:S(2)}) %collective-permute-start.6) | collective-permute-done | bytes 131104 | tf_op jit(solution)/shard_map/ppermute | solution.py:15
  75.7 2.2 %collective-permute-done.7 = bf16[1,256,2,128]{3,1,2,0:T(8,128)(2,1)S(1)} collective-permute-done((bf16[1,256,2,128]{3,1,2,0:T(8,128)(2,1)S(1)}, bf16[1,256,2,128]{3,1,2,0:T(8,128)(2,1)S(1)}, u32[]{:S(2)}, u32[]{:S(2)}) %collective-permute-start.7) | collective-permute-done | bytes 131104 | tf_op jit(solution)/shard_map/ppermute | solution.py:15
  77.9 0.3 fusion.24
  78.2 0.3 fusion.22
  78.4 0.3 fusion.20
  78.7 0.3 fusion.18
  79.0 0.3 fusion.16
  79.2 0.3 fusion.14
  79.5 0.3 fusion.12
  79.8 0.3 fusion.10
  80.0 0.0 copy-start
  80.1 1.4 %copy-done = bf16[9,1,2,256,256]{3,4,2,1,0:T(8,128)(2,1)} copy-done((bf16[9,1,2,256,256]{3,4,2,1,0:T(8,128)(2,1)}, bf16[9,1,2,256,256]{3,4,2,1,0:T(8,128)(2,1)S(1)}, u32[]{:S(2)}) %copy-start) | copy-done | bytes 2359320
  81.5 2.4 %gather_fusion = bf16[9,2,256,256]{2,3,1,0:T(8,128)(2,1)S(1)} fusion(bf16[9,2,256,256]{2,3,1,0:T(8,128)(2,1)} %bitcast.252, s32[1024]{0:T(1024)S(1)} %pad_clamp_fusion), kind=kCustom, calls=%fused_computation | custom fusion | bytes 4718628 | tf_op jit(solution)/shard_map/jit(_take)/gather | solution.py:75
  83.8 1.7 %bitcast_select_fusion = bf16[1,9,1,2,256,256]{4,5,3,1,2,0:T(8,128)(2,1)} fusion(bf16[9,2,256,256]{2,3,1,0:T(8,128)(2,1)S(1)} %gather_fusion, pred[9]{0:T(512)(128)(4,1)S(1)} %compare_and_fusion), kind=kLoop, calls=%fused_computation.1 | loop fusion | flops 1179648 | bytes 4718601 | tf_op jit(solution)/shard_map/jit(_take)/select_n | solution.py:75
  85.5 4.3 %copy.18 = bf16[1,9,1,2,256,256]{5,4,3,2,1,0:T(8,128)(2,1)} copy(bf16[1,9,1,2,256,256]{4,5,3,1,2,0:T(8,128)(2,1)} %bitcast_select_fusion) | data formatting | bytes 4718592 | tf_op jit(solution)/shard_map/jit(_take)/select_n | solution.py:75
  (33 shorter events, 0.5 us)
Async XLA Ops:
  3.1 3.7 %copy-start.1 = (f32[4,32]{1,0:T(4,128)S(1)}, f32[4,32]{1,0:T(4,128)}, u32[]{:S(2)}) copy-start(f32[4,32]{1,0:T(4,128)} %param.4) | copy-start | bytes 1540
  6.5 21.1 %copy-start.2 = (s32[1,9]{1,0:T(1,128)S(1)}, s32[1,9]{1,0:T(1,128)}, u32[]{:S(2)}) copy-start(s32[1,9]{1,0:T(1,128)} %param.5) | copy-start | bytes 112
  9.1 34.8 %all-to-all-start = ((bf16[32,8,2,128]{3,1,2,0:T(8,128)(2,1)}), bf16[32,8,2,128]{3,1,2,0:T(8,128)(2,1)S(1)}, u32[]{:S(2)}, u32[]{:S(2)}) async-start(bf16[32,8,2,128]{3,1,2,0:T(8,128)(2,1)} %copy.16), calls=%async_computation | async-start | bytes 262144 | tf_op jit(solution)/shard_map/all_to_all | solution.py:66
  44.0 20.2 %collective-permute-start = (bf16[1,256,2,128]{3,1,2,0:T(8,128)(2,1)S(1)}, bf16[1,256,2,128]{3,1,2,0:T(8,128)(2,1)S(1)}, u32[]{:S(2)}, u32[]{:S(2)}) collective-permute-start(bf16[1,256,2,128]{3,1,2,0:T(8,128)(2,1)S(1)} %bitcast.255), channel_id=1, source_target_pairs={{0,32},{32,64},{64,96},{96,128},{128,160},{160,192},{192,224},{224... | collective-permute-start | bytes 393224 | tf_op jit(solution)/shard_map/ppermute | solution.py:15
  50.1 17.0 %collective-permute-start.1 = (bf16[1,256,2,128]{3,1,2,0:T(8,128)(2,1)S(1)}, bf16[1,256,2,128]{3,1,2,0:T(8,128)(2,1)S(1)}, u32[]{:S(2)}, u32[]{:S(2)}) collective-permute-start(bf16[1,256,2,128]{3,1,2,0:T(8,128)(2,1)S(1)} %bitcast.256), channel_id=1, source_target_pairs={{0,64},{32,96},{64,128},{96,160},{128,192},{160,224},{192,256},{22... | collective-permute-start | bytes 393224 | tf_op jit(solution)/shard_map/ppermute | solution.py:15
  53.3 17.4 %collective-permute-start.2 = (bf16[1,256,2,128]{3,1,2,0:T(8,128)(2,1)S(1)}, bf16[1,256,2,128]{3,1,2,0:T(8,128)(2,1)S(1)}, u32[]{:S(2)}, u32[]{:S(2)}) collective-permute-start(bf16[1,256,2,128]{3,1,2,0:T(8,128)(2,1)S(1)} %bitcast.257), channel_id=1, source_target_pairs={{0,96},{32,128},{64,160},{96,192},{128,224},{160,256},{192,288},{2... | collective-permute-start | bytes 393224 | tf_op jit(solution)/shard_map/ppermute | solution.py:15
  56.8 17.0 %collective-permute-start.3 = (bf16[1,256,2,128]{3,1,2,0:T(8,128)(2,1)S(1)}, bf16[1,256,2,128]{3,1,2,0:T(8,128)(2,1)S(1)}, u32[]{:S(2)}, u32[]{:S(2)}) collective-permute-start(bf16[1,256,2,128]{3,1,2,0:T(8,128)(2,1)S(1)} %bitcast.258), channel_id=1, source_target_pairs={{0,128},{32,160},{64,192},{96,224},{128,256},{160,288},{192,320},{... | collective-permute-start | bytes 393224 | tf_op jit(solution)/shard_map/ppermute | solution.py:15
  59.1 14.8 %collective-permute-start.4 = (bf16[1,256,2,128]{3,1,2,0:T(8,128)(2,1)S(1)}, bf16[1,256,2,128]{3,1,2,0:T(8,128)(2,1)S(1)}, u32[]{:S(2)}, u32[]{:S(2)}) collective-permute-start(bf16[1,256,2,128]{3,1,2,0:T(8,128)(2,1)S(1)} %bitcast.259), channel_id=1, source_target_pairs={{0,160},{32,192},{64,224},{96,256},{128,288},{160,320},{192,352},{... | collective-permute-start | bytes 393224 | tf_op jit(solution)/shard_map/ppermute | solution.py:15
  64.1 9.9 %collective-permute-start.5 = (bf16[1,256,2,128]{3,1,2,0:T(8,128)(2,1)S(1)}, bf16[1,256,2,128]{3,1,2,0:T(8,128)(2,1)S(1)}, u32[]{:S(2)}, u32[]{:S(2)}) collective-permute-start(bf16[1,256,2,128]{3,1,2,0:T(8,128)(2,1)S(1)} %bitcast.260), channel_id=1, source_target_pairs={{0,192},{32,224},{64,256},{96,288},{128,320},{160,352},{192,384},{... | collective-permute-start | bytes 393224 | tf_op jit(solution)/shard_map/ppermute | solution.py:15
  67.0 8.5 %collective-permute-start.6 = (bf16[1,256,2,128]{3,1,2,0:T(8,128)(2,1)S(1)}, bf16[1,256,2,128]{3,1,2,0:T(8,128)(2,1)S(1)}, u32[]{:S(2)}, u32[]{:S(2)}) collective-permute-start(bf16[1,256,2,128]{3,1,2,0:T(8,128)(2,1)S(1)} %bitcast.261), channel_id=1, source_target_pairs={{0,224},{32,256},{64,288},{96,320},{128,352},{160,384},{192,416},{... | collective-permute-start | bytes 393224 | tf_op jit(solution)/shard_map/ppermute | solution.py:15
  70.7 7.1 %collective-permute-start.7 = (bf16[1,256,2,128]{3,1,2,0:T(8,128)(2,1)S(1)}, bf16[1,256,2,128]{3,1,2,0:T(8,128)(2,1)S(1)}, u32[]{:S(2)}, u32[]{:S(2)}) collective-permute-start(bf16[1,256,2,128]{3,1,2,0:T(8,128)(2,1)S(1)} %bitcast.262), channel_id=1, source_target_pairs={{0,256},{32,288},{64,320},{96,352},{128,384},{160,416},{192,448},{... | collective-permute-start | bytes 393224 | tf_op jit(solution)/shard_map/ppermute | solution.py:15
  80.0 1.4 %copy-start = (bf16[9,1,2,256,256]{3,4,2,1,0:T(8,128)(2,1)}, bf16[9,1,2,256,256]{3,4,2,1,0:T(8,128)(2,1)S(1)}, u32[]{:S(2)}) copy-start(bf16[9,1,2,256,256]{3,4,2,1,0:T(8,128)(2,1)S(1)} %fusion.10) | copy-start | bytes 7077892
where the time goes:
time: 90.4 us; the launch traced here: 89.8 us
  starting transfers between devices  47.8 us (53%)
  waiting for transfers between devices  19.9 us (22%)
  local copies, waits for them, and re-layouts  15.6 us (17%)
  matrix products  3.73 us (4%)
  other arithmetic  2.26 us (2%)
    ppermute x8, starting transfers between devices, shifted(): lax.ppermute(x, axis, [(i, (i + by) % length) for i in range(length)])  29.3 us
    all_to_all x1, starting transfers between devices, per_device(): lax.all_to_all(local_spectra, 'dev', split_axis=0, concat_axis=1, tiled=T...  18.5 us
    all_to_all x1, waiting for transfers between devices, per_device(): lax.all_to_all(local_spectra, 'dev', split_axis=0, concat_axis=1, tiled=T...  16.3 us
    unnamed x10, local copies, waits for them, and re-layouts  5.1 us
    select_n x1, local copies, waits for them, and re-layouts, per_device(): return jnp.take(stacked, plan[0], axis=0)[None]  4.26 us
    ppermute x8, waiting for transfers between devices, shifted(): lax.ppermute(x, axis, [(i, (i + by) % length) for i in range(length)])  3.6 us
    gather x1, local copies, waits for them, and re-layouts, per_device(): return jnp.take(stacked, plan[0], axis=0)[None]  2.36 us
    dot_general x9, matrix products, correlate(): jnp.einsum('gzi,gkvi->gkzv', left_spectrum_rows, right_spectrum_rows, pre...  2.35 us
  transfers between devices with their start and end apart: 9, of which 3 were waited for; matrix products, arithmetic and copies ran while one was open for 1% of the time, Pallas kernels for 0%

commit v1 on v0

--- a/solution.py
+++ b/solution.py
@@ -63,7 +63,10 @@
 
 def per_device(voltage, filter_taps, plan):
     local_spectra = compute_spectra(voltage, filter_taps)
-    own_block = lax.all_to_all(local_spectra, "dev", split_axis=0, concat_axis=1, tiled=True)
+    size = lax.axis_size("dev")
+    pieces = jnp.stack(jnp.split(local_spectra, size, axis=0), axis=0)
+    pieces = lax.all_to_all(pieces, "dev", split_axis=0, concat_axis=0)
+    own_block = jnp.concatenate(pieces, axis=1)
     groups = lax.axis_size("grp")
     rounds = groups // 2 + 1
     results = [correlate(own_block, own_block)]

time: 90.4 us -> 106 us (1.17)
  local copies, waits for them, and re-layouts: 15.6 us -> 29.3 us
  matrix products: 3.73 us -> 5.17 us
    unnamed x10 -> x35, local copies, waits for them, and re-layouts: 5.1 us -> 19.8 us
    slice x1 -> x0, local copies, waits for them, and re-layouts: 1.77 us -> none  [compute_spectra(): framed_samples[:, :, 0:SPECTRA, :]]
where the time goes in v1:
time: 106 us
  starting transfers between devices  47.8 us (45%)
  local copies, waits for them, and re-layouts  29.3 us (28%)
  waiting for transfers between devices  19.9 us (19%)
  matrix products  5.17 us (5%)
  other arithmetic  2.88 us (3%)
    ppermute x8, starting transfers between devices, shifted(): lax.ppermute(x, axis, [(i, (i + by) % length) for i in range(length)])  29.3 us
    unnamed x35, local copies, waits for them, and re-layouts  19.8 us
    all_to_all x1, starting transfers between devices, per_device(): pieces = lax.all_to_all(pieces, 'dev', split_axis=0, concat_axis=0)  18.5 us
    all_to_all x1, waiting for transfers between devices, per_device(): pieces = lax.all_to_all(pieces, 'dev', split_axis=0, concat_axis=0)  16.3 us
    select_n x1, local copies, waits for them, and re-layouts, per_device(): return jnp.take(stacked, plan[0], axis=0)[None]  4.26 us
    ppermute x8, waiting for transfers between devices, shifted(): lax.ppermute(x, axis, [(i, (i + by) % length) for i in range(length)])  3.61 us
    gather x1, local copies, waits for them, and re-layouts, per_device(): return jnp.take(stacked, plan[0], axis=0)[None]  2.36 us
    dot_general x9, matrix products, correlate(): jnp.einsum('gzi,gkvi->gkzv', left_spectrum_rows, right_spectrum_rows, pre...  2.36 us
  transfers between devices with their start and end apart: 9, of which 3 were waited for; matrix products, arithmetic and copies ran while one was open for 1% of the time, Pallas kernels for 0%

profile of v1, /device:TPU:1, one launch (start us, length us, event | category | flops | bytes accessed | tf_op | source)
XLA Modules:
  0.0 105.5 jit_solution(4229521097712392980)
XLA Ops:
  0.0 1.3 %reshape.247 = f32[2,8,131,32]{3,2,1,0:T(8,128)S(1)} reshape(f32[2,8,4192]{2,1,0:T(8,128)} %param.3) | data formatting | bytes 536576 | tf_op jit(solution)/shard_map/reshape | solution.py:20
  1.3 0.8 slice_bitcast_fusion.27
  2.2 0.4 fusion.31
  2.6 0.7 fusion.35
  3.3 0.7 fusion.34
  4.0 0.7 fusion.29
  4.7 0.7 fusion.30
  5.8 0.6 constant_dynamic-update-slice_fusion.31
  6.4 0.6 constant_dynamic-update-slice_fusion.30
  7.0 0.6 constant_dynamic-update-slice_fusion.29
  7.6 0.6 constant_dynamic-update-slice_fusion.28
  8.2 0.6 constant_dynamic-update-slice_fusion.27
  8.8 0.6 constant_dynamic-update-slice_fusion.26
  9.4 0.6 constant_dynamic-update-slice_fusion.25
  10.0 0.6 constant_dynamic-update-slice_fusion.24
  10.6 0.6 constant_dynamic-update-slice_fusion.23
  11.2 0.6 constant_dynamic-update-slice_fusion.22
  11.8 0.6 constant_dynamic-update-slice_fusion.21
  12.3 0.6 constant_dynamic-update-slice_fusion.20
  12.9 0.6 constant_dynamic-update-slice_fusion.19
  13.5 0.6 constant_dynamic-update-slice_fusion.18
  14.1 0.6 constant_dynamic-update-slice_fusion.17
  14.7 0.6 constant_dynamic-update-slice_fusion.16
  15.3 0.6 constant_dynamic-update-slice_fusion.15
  15.9 0.6 constant_dynamic-update-slice_fusion.14
  16.5 0.6 constant_dynamic-update-slice_fusion.13
  17.1 0.6 constant_dynamic-update-slice_fusion.12
  17.7 0.6 constant_dynamic-update-slice_fusion.11
  18.3 0.6 constant_dynamic-update-slice_fusion.10
  18.9 0.6 constant_dynamic-update-slice_fusion.9
  19.5 0.6 constant_dynamic-update-slice_fusion.8
  20.1 0.6 constant_dynamic-update-slice_fusion.7
  20.7 0.6 constant_dynamic-update-slice_fusion.6
  21.3 0.6 constant_dynamic-update-slice_fusion.5
  21.9 0.6 constant_dynamic-update-slice_fusion.4
  22.5 0.6 constant_dynamic-update-slice_fusion.3
  23.1 0.6 constant_dynamic-update-slice_fusion.2
  23.6 0.6 constant_dynamic-update-slice_fusion.1
  24.2 0.6 constant_dynamic-update-slice_fusion
  24.8 18.5 %all-to-all-start = ((bf16[32,1,8,2,128]{4,2,3,1,0:T(8,128)(2,1)}), bf16[32,1,8,2,128]{4,2,3,1,0:T(8,128)(2,1)S(1)}, u32[]{:S(2)}, u32[]{:S(2)}) async-start(bf16[32,1,8,2,128]{4,2,3,1,0:T(8,128)(2,1)} %constant_dynamic-update-slice_fusion), calls=%async_computation | async-start | bytes 262144 | tf_op jit(solution)/shard_map/all_to_all | solution.py:68
  43.4 16.3 %all-to-all-done = bf16[32,1,8,2,128]{4,2,3,1,0:T(8,128)(2,1)S(1)} async-done(((bf16[32,1,8,2,128]{4,2,3,1,0:T(8,128)(2,1)}), bf16[32,1,8,2,128]{4,2,3,1,0:T(8,128)(2,1)S(1)}, u32[]{:S(2)}, u32[]{:S(2)}) %all-to-all-start) | async-done | bytes 131104 | tf_op jit(solution)/shard_map/all_to_all | solution.py:68
  59.7 6.1 %collective-permute-start = (bf16[1,256,2,128]{3,1,2,0:T(8,128)(2,1)S(1)}, bf16[1,256,2,128]{3,1,2,0:T(8,128)(2,1)S(1)}, u32[]{:S(2)}, u32[]{:S(2)}) collective-permute-start(bf16[1,256,2,128]{3,1,2,0:T(8,128)(2,1)S(1)} %bitcast.323), channel_id=1, source_target_pairs={{0,32},{32,64},{64,96},{96,128},{128,160},{160,192},{192,224},{224... | collective-permute-start | bytes 393224 | tf_op jit(solution)/shard_map/ppermute | solution.py:15
  65.8 3.2 %collective-permute-start.1 = (bf16[1,256,2,128]{3,1,2,0:T(8,128)(2,1)S(1)}, bf16[1,256,2,128]{3,1,2,0:T(8,128)(2,1)S(1)}, u32[]{:S(2)}, u32[]{:S(2)}) collective-permute-start(bf16[1,256,2,128]{3,1,2,0:T(8,128)(2,1)S(1)} %bitcast.324), channel_id=1, source_target_pairs={{0,64},{32,96},{64,128},{96,160},{128,192},{160,224},{192,256},{22... | collective-permute-start | bytes 393224 | tf_op jit(solution)/shard_map/ppermute | solution.py:15
  69.0 3.5 %collective-permute-start.2 = (bf16[1,256,2,128]{3,1,2,0:T(8,128)(2,1)S(1)}, bf16[1,256,2,128]{3,1,2,0:T(8,128)(2,1)S(1)}, u32[]{:S(2)}, u32[]{:S(2)}) collective-permute-start(bf16[1,256,2,128]{3,1,2,0:T(8,128)(2,1)S(1)} %bitcast.325), channel_id=1, source_target_pairs={{0,96},{32,128},{64,160},{96,192},{128,224},{160,256},{192,288},{2... | collective-permute-start | bytes 393224 | tf_op jit(solution)/shard_map/ppermute | solution.py:15
  72.5 2.3 %collective-permute-start.3 = (bf16[1,256,2,128]{3,1,2,0:T(8,128)(2,1)S(1)}, bf16[1,256,2,128]{3,1,2,0:T(8,128)(2,1)S(1)}, u32[]{:S(2)}, u32[]{:S(2)}) collective-permute-start(bf16[1,256,2,128]{3,1,2,0:T(8,128)(2,1)S(1)} %bitcast.326), channel_id=1, source_target_pairs={{0,128},{32,160},{64,192},{96,224},{128,256},{160,288},{192,320},{... | collective-permute-start | bytes 393224 | tf_op jit(solution)/shard_map/ppermute | solution.py:15
  74.8 4.7 %collective-permute-start.4 = (bf16[1,256,2,128]{3,1,2,0:T(8,128)(2,1)S(1)}, bf16[1,256,2,128]{3,1,2,0:T(8,128)(2,1)S(1)}, u32[]{:S(2)}, u32[]{:S(2)}) collective-permute-start(bf16[1,256,2,128]{3,1,2,0:T(8,128)(2,1)S(1)} %bitcast.327), channel_id=1, source_target_pairs={{0,160},{32,192},{64,224},{96,256},{128,288},{160,320},{192,352},{... | collective-permute-start | bytes 393224 | tf_op jit(solution)/shard_map/ppermute | solution.py:15
  79.6 0.3 fusion.26
  79.8 2.8 %collective-permute-start.5 = (bf16[1,256,2,128]{3,1,2,0:T(8,128)(2,1)S(1)}, bf16[1,256,2,128]{3,1,2,0:T(8,128)(2,1)S(1)}, u32[]{:S(2)}, u32[]{:S(2)}) collective-permute-start(bf16[1,256,2,128]{3,1,2,0:T(8,128)(2,1)S(1)} %bitcast.328), channel_id=1, source_target_pairs={{0,192},{32,224},{64,256},{96,288},{128,320},{160,352},{192,384},{... | collective-permute-start | bytes 393224 | tf_op jit(solution)/shard_map/ppermute | solution.py:15
  82.7 3.6 %collective-permute-start.6 = (bf16[1,256,2,128]{3,1,2,0:T(8,128)(2,1)S(1)}, bf16[1,256,2,128]{3,1,2,0:T(8,128)(2,1)S(1)}, u32[]{:S(2)}, u32[]{:S(2)}) collective-permute-start(bf16[1,256,2,128]{3,1,2,0:T(8,128)(2,1)S(1)} %bitcast.329), channel_id=1, source_target_pairs={{0,224},{32,256},{64,288},{96,320},{128,352},{160,384},{192,416},{... | collective-permute-start | bytes 393224 | tf_op jit(solution)/shard_map/ppermute | solution.py:15
  86.4 3.1 %collective-permute-start.7 = (bf16[1,256,2,128]{3,1,2,0:T(8,128)(2,1)S(1)}, bf16[1,256,2,128]{3,1,2,0:T(8,128)(2,1)S(1)}, u32[]{:S(2)}, u32[]{:S(2)}) collective-permute-start(bf16[1,256,2,128]{3,1,2,0:T(8,128)(2,1)S(1)} %bitcast.330), channel_id=1, source_target_pairs={{0,256},{32,288},{64,320},{96,352},{128,384},{160,416},{192,448},{... | collective-permute-start | bytes 393224 | tf_op jit(solution)/shard_map/ppermute | solution.py:15
  89.9 1.4 %collective-permute-done.6 = bf16[1,256,2,128]{3,1,2,0:T(8,128)(2,1)S(1)} collective-permute-done((bf16[1,256,2,128]{3,1,2,0:T(8,128)(2,1)S(1)}, bf16[1,256,2,128]{3,1,2,0:T(8,128)(2,1)S(1)}, u32[]{:S(2)}, u32[]{:S(2)}) %collective-permute-start.6) | collective-permute-done | bytes 131104 | tf_op jit(solution)/shard_map/ppermute | solution.py:15
  91.4 2.2 %collective-permute-done.7 = bf16[1,256,2,128]{3,1,2,0:T(8,128)(2,1)S(1)} collective-permute-done((bf16[1,256,2,128]{3,1,2,0:T(8,128)(2,1)S(1)}, bf16[1,256,2,128]{3,1,2,0:T(8,128)(2,1)S(1)}, u32[]{:S(2)}, u32[]{:S(2)}) %collective-permute-start.7) | collective-permute-done | bytes 131104 | tf_op jit(solution)/shard_map/ppermute | solution.py:15
  93.6 0.3 fusion.24
  93.9 0.3 fusion.22
  94.2 0.3 fusion.20
  94.4 0.3 fusion.18
  94.7 0.3 fusion.16
  95.0 0.3 fusion.14
  95.2 0.3 fusion.12
  95.5 0.3 fusion.10
  95.8 1.4 %copy-done = bf16[9,1,2,256,256]{3,4,2,1,0:T(8,128)(2,1)} copy-done((bf16[9,1,2,256,256]{3,4,2,1,0:T(8,128)(2,1)}, bf16[9,1,2,256,256]{3,4,2,1,0:T(8,128)(2,1)S(1)}, u32[]{:S(2)}) %copy-start) | copy-done | bytes 2359320
  97.2 2.4 %gather_fusion = bf16[9,2,256,256]{2,3,1,0:T(8,128)(2,1)S(1)} fusion(bf16[9,2,256,256]{2,3,1,0:T(8,128)(2,1)} %bitcast.320, s32[1024]{0:T(1024)S(1)} %pad_clamp_fusion), kind=kCustom, calls=%fused_computation | custom fusion | bytes 4718628 | tf_op jit(solution)/shard_map/jit(_take)/gather | solution.py:78
  99.6 1.7 %bitcast_select_fusion = bf16[1,9,1,2,256,256]{4,5,3,1,2,0:T(8,128)(2,1)} fusion(bf16[9,2,256,256]{2,3,1,0:T(8,128)(2,1)S(1)} %gather_fusion, pred[9]{0:T(512)(128)(4,1)S(1)} %compare_and_fusion), kind=kLoop, calls=%fused_computation.1 | loop fusion | flops 1179648 | bytes 4718601 | tf_op jit(solution)/shard_map/jit(_take)/select_n | solution.py:78
  101.3 4.3 %copy.684 = bf16[1,9,1,2,256,256]{5,4,3,2,1,0:T(8,128)(2,1)} copy(bf16[1,9,1,2,256,256]{4,5,3,1,2,0:T(8,128)(2,1)} %bitcast_select_fusion) | data formatting | bytes 4718592 | tf_op jit(solution)/shard_map/jit(_take)/select_n | solution.py:78
  (44 shorter events, 0.9 us)
Async XLA Ops:
  2.6 40.7 %copy-start.1 = (s32[1,9]{1,0:T(1,128)S(1)}, s32[1,9]{1,0:T(1,128)}, u32[]{:S(2)}) copy-start(s32[1,9]{1,0:T(1,128)} %param.5) | copy-start | bytes 112
  24.8 34.8 %all-to-all-start = ((bf16[32,1,8,2,128]{4,2,3,1,0:T(8,128)(2,1)}), bf16[32,1,8,2,128]{4,2,3,1,0:T(8,128)(2,1)S(1)}, u32[]{:S(2)}, u32[]{:S(2)}) async-start(bf16[32,1,8,2,128]{4,2,3,1,0:T(8,128)(2,1)} %constant_dynamic-update-slice_fusion), calls=%async_computation | async-start | bytes 262144 | tf_op jit(solution)/shard_map/all_to_all | solution.py:68
  59.7 20.2 %collective-permute-start = (bf16[1,256,2,128]{3,1,2,0:T(8,128)(2,1)S(1)}, bf16[1,256,2,128]{3,1,2,0:T(8,128)(2,1)S(1)}, u32[]{:S(2)}, u32[]{:S(2)}) collective-permute-start(bf16[1,256,2,128]{3,1,2,0:T(8,128)(2,1)S(1)} %bitcast.323), channel_id=1, source_target_pairs={{0,32},{32,64},{64,96},{96,128},{128,160},{160,192},{192,224},{224... | collective-permute-start | bytes 393224 | tf_op jit(solution)/shard_map/ppermute | solution.py:15
  65.8 16.9 %collective-permute-start.1 = (bf16[1,256,2,128]{3,1,2,0:T(8,128)(2,1)S(1)}, bf16[1,256,2,128]{3,1,2,0:T(8,128)(2,1)S(1)}, u32[]{:S(2)}, u32[]{:S(2)}) collective-permute-start(bf16[1,256,2,128]{3,1,2,0:T(8,128)(2,1)S(1)} %bitcast.324), channel_id=1, source_target_pairs={{0,64},{32,96},{64,128},{96,160},{128,192},{160,224},{192,256},{22... | collective-permute-start | bytes 393224 | tf_op jit(solution)/shard_map/ppermute | solution.py:15
  69.0 17.4 %collective-permute-start.2 = (bf16[1,256,2,128]{3,1,2,0:T(8,128)(2,1)S(1)}, bf16[1,256,2,128]{3,1,2,0:T(8,128)(2,1)S(1)}, u32[]{:S(2)}, u32[]{:S(2)}) collective-permute-start(bf16[1,256,2,128]{3,1,2,0:T(8,128)(2,1)S(1)} %bitcast.325), channel_id=1, source_target_pairs={{0,96},{32,128},{64,160},{96,192},{128,224},{160,256},{192,288},{2... | collective-permute-start | bytes 393224 | tf_op jit(solution)/shard_map/ppermute | solution.py:15
  72.5 17.0 %collective-permute-start.3 = (bf16[1,256,2,128]{3,1,2,0:T(8,128)(2,1)S(1)}, bf16[1,256,2,128]{3,1,2,0:T(8,128)(2,1)S(1)}, u32[]{:S(2)}, u32[]{:S(2)}) collective-permute-start(bf16[1,256,2,128]{3,1,2,0:T(8,128)(2,1)S(1)} %bitcast.326), channel_id=1, source_target_pairs={{0,128},{32,160},{64,192},{96,224},{128,256},{160,288},{192,320},{... | collective-permute-start | bytes 393224 | tf_op jit(solution)/shard_map/ppermute | solution.py:15
  74.8 14.8 %collective-permute-start.4 = (bf16[1,256,2,128]{3,1,2,0:T(8,128)(2,1)S(1)}, bf16[1,256,2,128]{3,1,2,0:T(8,128)(2,1)S(1)}, u32[]{:S(2)}, u32[]{:S(2)}) collective-permute-start(bf16[1,256,2,128]{3,1,2,0:T(8,128)(2,1)S(1)} %bitcast.327), channel_id=1, source_target_pairs={{0,160},{32,192},{64,224},{96,256},{128,288},{160,320},{192,352},{... | collective-permute-start | bytes 393224 | tf_op jit(solution)/shard_map/ppermute | solution.py:15
  79.8 9.9 %collective-permute-start.5 = (bf16[1,256,2,128]{3,1,2,0:T(8,128)(2,1)S(1)}, bf16[1,256,2,128]{3,1,2,0:T(8,128)(2,1)S(1)}, u32[]{:S(2)}, u32[]{:S(2)}) collective-permute-start(bf16[1,256,2,128]{3,1,2,0:T(8,128)(2,1)S(1)} %bitcast.328), channel_id=1, source_target_pairs={{0,192},{32,224},{64,256},{96,288},{128,320},{160,352},{192,384},{... | collective-permute-start | bytes 393224 | tf_op jit(solution)/shard_map/ppermute | solution.py:15
  82.7 8.5 %collective-permute-start.6 = (bf16[1,256,2,128]{3,1,2,0:T(8,128)(2,1)S(1)}, bf16[1,256,2,128]{3,1,2,0:T(8,128)(2,1)S(1)}, u32[]{:S(2)}, u32[]{:S(2)}) collective-permute-start(bf16[1,256,2,128]{3,1,2,0:T(8,128)(2,1)S(1)} %bitcast.329), channel_id=1, source_target_pairs={{0,224},{32,256},{64,288},{96,320},{128,352},{160,384},{192,416},{... | collective-permute-start | bytes 393224 | tf_op jit(solution)/shard_map/ppermute | solution.py:15
  86.4 7.1 %collective-permute-start.7 = (bf16[1,256,2,128]{3,1,2,0:T(8,128)(2,1)S(1)}, bf16[1,256,2,128]{3,1,2,0:T(8,128)(2,1)S(1)}, u32[]{:S(2)}, u32[]{:S(2)}) collective-permute-start(bf16[1,256,2,128]{3,1,2,0:T(8,128)(2,1)S(1)} %bitcast.330), channel_id=1, source_target_pairs={{0,256},{32,288},{64,320},{96,352},{128,384},{160,416},{192,448},{... | collective-permute-start | bytes 393224 | tf_op jit(solution)/shard_map/ppermute | solution.py:15
  95.8 1.4 %copy-start = (bf16[9,1,2,256,256]{3,4,2,1,0:T(8,128)(2,1)}, bf16[9,1,2,256,256]{3,4,2,1,0:T(8,128)(2,1)S(1)}, u32[]{:S(2)}) copy-start(bf16[9,1,2,256,256]{3,4,2,1,0:T(8,128)(2,1)S(1)} %fusion.10) | copy-start | bytes 7077892
